TPU v7x, 32 devices: a whole 2x2x4 slice. The times are simulated.
32 devices in a mesh: fsdp: 2 (over x), ctx: 4 (over z), tp: 4 (over y, core).
Axes of the slice: x: 2, y: 2, z: 4, core: 2. Of those that a mesh axis runs over, the one named last changes fastest.
Arguments:
- tokens: bfloat16 [4, 2048, 2048], P('fsdp', 'ctx'), may hold values from -6 to 6
- tree_position: int32 [4, 2048], P('fsdp', 'ctx'), may hold values from 0 to 2047, as said below
- segment: int32 [4, 2048], P('fsdp', 'ctx'), may hold values from 0 to 6, as said below
- parent_table: int32 [4, 7], P('fsdp'), may hold values from 0 to 2, as said below
- norm1_gain: float32 [2048], replicated, may hold values from 0.5 to 1.5
- norm1_shift: float32 [2048], replicated, may hold values from -4 to 4
- query_weight: bfloat16 [2048, 2048], P('fsdp', 'tp'), may hold values from -0.125 to 0.125
- query_bias: float32 [2048], P('tp'), may hold values from -4 to 4
- key_weight: bfloat16 [2048, 2048], P('fsdp', 'tp'), may hold values from -0.125 to 0.125
- value_weight: bfloat16 [2048, 2048], P('fsdp', 'tp'), may hold values from -0.125 to 0.125
- value_bias: float32 [2048], P('tp'), may hold values from -0.75 to 0.75
- out_weight: bfloat16 [2048, 2048], P('tp', 'fsdp'), may hold values from -1.5 to 1.5
- out_bias: float32 [2048], replicated, may hold values from -4 to 4
- norm2_gain: float32 [2048], replicated, may hold values from 0.5 to 1.5
- norm2_shift: float32 [2048], replicated, may hold values from -4 to 4
- up_weight: bfloat16 [2048, 8192], P('fsdp', 'tp'), may hold values from -0.125 to 0.125
- up_bias: float32 [8192], P('tp'), may hold values from -4 to 4
- down_weight: bfloat16 [8192, 2048], P('tp', 'fsdp'), may hold values from -0.0625 to 0.0625
- down_bias: float32 [2048], replicated, may hold values from -4 to 4
- cotangent: bfloat16 [4, 2048, 2048], P('fsdp', 'ctx'), may hold values from -6 to 6
Outputs:
- layer_out: bfloat16 [4, 2048, 2048], P('fsdp', 'ctx')
- grad_tokens: bfloat16 [4, 2048, 2048], P('fsdp', 'ctx')
- grad_norm1_gain: float32 [2048], P(('fsdp', 'ctx'))
- grad_norm1_shift: float32 [2048], P(('fsdp', 'ctx'))
- grad_query_weight: float32 [2048, 2048], P(('fsdp', 'ctx'), 'tp')
- grad_query_bias: float32 [2048], P('tp')
- grad_key_weight: float32 [2048, 2048], P(('fsdp', 'ctx'), 'tp')
- grad_value_weight: float32 [2048, 2048], P(('fsdp', 'ctx'), 'tp')
- grad_value_bias: float32 [2048], P('tp')
- grad_out_weight: float32 [2048, 2048], P('tp', ('fsdp', 'ctx'))
- grad_out_bias: float32 [2048], P(('fsdp', 'ctx'))
- grad_norm2_gain: float32 [2048], P(('fsdp', 'ctx'))
- grad_norm2_shift: float32 [2048], P(('fsdp', 'ctx'))
- grad_up_weight: float32 [2048, 8192], P(('fsdp', 'ctx'), 'tp')
- grad_up_bias: float32 [8192], P('tp')
- grad_down_weight: float32 [8192, 2048], P('tp', ('fsdp', 'ctx'))
- grad_down_bias: float32 [2048], P(('fsdp', 'ctx'))
Inputs may be any that keep to these rules, and one draw needn't show every extreme that they name: `tree_position`: within each tree the rows hold the positions 0 to 2047 once each; every aligned run of 64 rows holds 64 consecutive positions in increasing order. `segment`: along increasing positions a tree runs through segments 0 to 6 in order, each nonempty and contiguous: the trunk 0 with 1024 positions, branches 1 and 2 with 512 together, leaves 3 to 6 with 512 together. `parent_table`: entry s of a tree's row is the parent of segment s: 0 for segments 0, 1 and 2; 1 for leaf 3; 2 for leaf 6; 1 or 2 for leaves 4 and 5.
All inputs are finite; a program needn't handle non-finite values.
Results may differ from a plain program's by a relative error of at most 0.024.
Values may be sent and summed in bfloat16 or wider, within the bound.
No kernel may reach another device: no remote copies, remote signals or barrier semaphores. Data moves between devices by JAX's collectives and lax.ppermute only.
A program may use at most 256 MiB of HBM per device.

v0:
```python
from functools import partial
import math
import jax
import jax.numpy as jnp
from jax import lax
from jax.sharding import PartitionSpec as P

HD = 128
NEGATIVE = -1000000000.0


def norm_rows(values, gain, shift):
    centre = jnp.mean(values, axis=-1, keepdims=True)
    centred = values - centre
    spread = jnp.mean(centred * centred, axis=-1, keepdims=True)
    return centred * lax.rsqrt(spread + 1e-05) * gain + shift


def on_path(query_pos, query_seg, key_pos, key_seg, parent):
    labels = jnp.arange(parent.shape[0], dtype=jnp.int32)
    first = jnp.sum(jnp.where(query_seg[:, None] == labels[None, :], parent[None, :], 0), axis=1)
    second = jnp.sum(jnp.where(first[:, None] == labels[None, :], parent[None, :], 0), axis=1)
    along = (
        (key_seg[None, :] == query_seg[:, None])
        | (key_seg[None, :] == first[:, None])
        | (key_seg[None, :] == second[:, None])
    )
    return along & (key_pos[None, :] <= query_pos[:, None])


def inner_rows(left, right):
    return lax.dot_general(
        left, right, (((0,), (0,)), ((), ())), preferred_element_type=jnp.float32
    )


def times_transposed(left, right):
    return lax.dot_general(
        left, right, (((1,), (1,)), ((), ())), preferred_element_type=jnp.float32
    )


def per_device(
    tokens,
    tree_position,
    segment,
    parent_table,
    norm1_gain,
    norm1_shift,
    query_weight,
    query_bias,
    key_weight,
    value_weight,
    value_bias,
    out_weight,
    out_bias,
    norm2_gain,
    norm2_shift,
    up_weight,
    up_bias,
    down_weight,
    down_bias,
    cotangent,
):
    w_query, w_key, w_value, w_out, w_up, w_down = (
        lax.all_gather(query_weight, "fsdp", axis=0, tiled=True),
        lax.all_gather(key_weight, "fsdp", axis=0, tiled=True),
        lax.all_gather(value_weight, "fsdp", axis=0, tiled=True),
        lax.all_gather(out_weight, "fsdp", axis=1, tiled=True),
        lax.all_gather(up_weight, "fsdp", axis=0, tiled=True),
        lax.all_gather(down_weight, "fsdp", axis=1, tiled=True),
    )
    key_position, key_segment = (
        lax.all_gather(tree_position, "ctx", axis=1, tiled=True),
        lax.all_gather(segment, "ctx", axis=1, tiled=True),
    )
    local_width = w_query.shape[1]
    head_count = local_width // HD
    score_scale = 1.0 / math.sqrt(HD)
    gelu_exact = partial(jax.nn.gelu, approximate=False)
    layer_rows = []
    input_grads = []
    running = [
        jnp.zeros(w_query.shape, jnp.float32),
        jnp.zeros(w_key.shape, jnp.float32),
        jnp.zeros(w_value.shape, jnp.float32),
        jnp.zeros(w_out.shape, jnp.float32),
        jnp.zeros(w_up.shape, jnp.float32),
        jnp.zeros(w_down.shape, jnp.float32),
        jnp.zeros(norm1_gain.shape, jnp.float32),
        jnp.zeros(norm1_shift.shape, jnp.float32),
        jnp.zeros(norm2_gain.shape, jnp.float32),
        jnp.zeros(norm2_shift.shape, jnp.float32),
        jnp.zeros(out_bias.shape, jnp.float32),
        jnp.zeros(down_bias.shape, jnp.float32),
    ]
    head_sums = [
        jnp.zeros(query_bias.shape, jnp.float32),
        jnp.zeros(value_bias.shape, jnp.float32),
        jnp.zeros(up_bias.shape, jnp.float32),
    ]
    for batch_index in range(tokens.shape[0]):
        inputs = tokens[batch_index].astype(jnp.float32)
        local_rows = inputs.shape[0]
        normed = norm_rows(inputs, norm1_gain, norm1_shift).astype(jnp.bfloat16)
        queries = (
            jnp.dot(normed, w_query, preferred_element_type=jnp.float32) + query_bias
        ).astype(jnp.bfloat16)
        keys_local = jnp.dot(normed, w_key, preferred_element_type=jnp.float32).astype(jnp.bfloat16)
        values_local = (
            jnp.dot(normed, w_value, preferred_element_type=jnp.float32) + value_bias
        ).astype(jnp.bfloat16)
        keys_tree, values_tree = (
            lax.all_gather(keys_local, "ctx", axis=0, tiled=True),
            lax.all_gather(values_local, "ctx", axis=0, tiled=True),
        )
        tree_rows = keys_tree.shape[0]
        visible = on_path(
            tree_position[batch_index],
            segment[batch_index],
            key_position[batch_index],
            key_segment[batch_index],
            parent_table[batch_index],
        )
        query_heads = queries.reshape(local_rows, head_count, HD)
        key_heads = keys_tree.reshape(tree_rows, head_count, HD)
        value_heads = values_tree.reshape(tree_rows, head_count, HD)
        scores = (
            jnp.einsum("qhd,khd->hqk", query_heads, key_heads, preferred_element_type=jnp.float32)
            * score_scale
        )
        scores = jnp.where(visible[None], scores, NEGATIVE)
        row_max = jnp.max(scores, axis=-1, keepdims=True)
        shifted = jnp.exp(scores - row_max)
        row_total = jnp.sum(shifted, axis=-1, keepdims=True)
        log_total = row_max + jnp.log(row_total)
        soft_low = (shifted / row_total).astype(jnp.bfloat16)
        attended = (
            jnp.einsum("hqk,khd->qhd", soft_low, value_heads, preferred_element_type=jnp.float32)
            .reshape(local_rows, local_width)
            .astype(jnp.bfloat16)
        )
        middle = inputs + (
            lax.psum(
                jnp.dot(attended, w_out, preferred_element_type=jnp.float32).astype(jnp.bfloat16),
                "tp",
            ).astype(jnp.float32)
            + out_bias
        )
        normed_mid = norm_rows(middle, norm2_gain, norm2_shift).astype(jnp.bfloat16)
        hidden = jnp.dot(normed_mid, w_up, preferred_element_type=jnp.float32) + up_bias
        active = gelu_exact(hidden).astype(jnp.bfloat16)
        result = middle + (
            lax.psum(
                jnp.dot(active, w_down, preferred_element_type=jnp.float32).astype(jnp.bfloat16),
                "tp",
            ).astype(jnp.float32)
            + down_bias
        )
        layer_rows.append(result.astype(jnp.bfloat16))
        grad_out = cotangent[batch_index]
        grad_float = grad_out.astype(jnp.float32)
        down_bias_term = jnp.sum(grad_float, axis=0)
        down_term = inner_rows(active, grad_out)
        _, gelu_pull = jax.vjp(gelu_exact, hidden)
        grad_hidden = gelu_pull(times_transposed(grad_out, w_down))[0].astype(jnp.bfloat16)
        up_bias_term = jnp.sum(grad_hidden.astype(jnp.float32), axis=0)
        up_term = inner_rows(normed_mid, grad_hidden)
        grad_normed_mid = lax.psum(
            times_transposed(grad_hidden, w_up).astype(jnp.bfloat16), "tp"
        ).astype(jnp.float32)
        _, second_pull = jax.vjp(norm_rows, middle, norm2_gain, norm2_shift)
        grad_mid_norm, second_gain_term, second_shift_term = second_pull(grad_normed_mid)
        grad_middle = grad_float + grad_mid_norm
        grad_branch = grad_middle.astype(jnp.bfloat16)
        out_bias_term = jnp.sum(grad_branch.astype(jnp.float32), axis=0)
        out_term = inner_rows(attended, grad_branch)
        grad_attended = times_transposed(grad_branch, w_out).astype(jnp.bfloat16)
        grad_heads = grad_attended.reshape(local_rows, head_count, HD)
        again = (
            jnp.einsum("qhd,khd->hqk", query_heads, key_heads, preferred_element_type=jnp.float32)
            * score_scale
        )
        again = jnp.where(visible[None], again, NEGATIVE)
        soft = jnp.exp(again - log_total)
        soft_again = soft.astype(jnp.bfloat16)
        grad_soft = jnp.einsum(
            "qhd,khd->hqk", grad_heads, value_heads, preferred_element_type=jnp.float32
        )
        inner = jnp.sum(soft * grad_soft, axis=-1, keepdims=True)
        grad_scores = (soft * (grad_soft - inner)).astype(jnp.bfloat16)
        grad_queries = (
            (
                jnp.einsum(
                    "hqk,khd->qhd", grad_scores, key_heads, preferred_element_type=jnp.float32
                )
                * score_scale
            )
            .reshape(local_rows, local_width)
            .astype(jnp.bfloat16)
        )
        key_part = (
            jnp.einsum("hqk,qhd->khd", grad_scores, query_heads, preferred_element_type=jnp.float32)
            * score_scale
        ).reshape(tree_rows, local_width)
        value_part = jnp.einsum(
            "hqk,qhd->khd", soft_again, grad_heads, preferred_element_type=jnp.float32
        ).reshape(tree_rows, local_width)
        grad_keys, grad_values = (
            lax.psum_scatter(
                key_part.astype(jnp.bfloat16), "ctx", scatter_dimension=0, tiled=True
            ).astype(jnp.float32),
            lax.psum_scatter(
                value_part.astype(jnp.bfloat16), "ctx", scatter_dimension=0, tiled=True
            ).astype(jnp.float32),
        )
        grad_keys = grad_keys.astype(jnp.bfloat16)
        grad_values = grad_values.astype(jnp.bfloat16)
        query_bias_term = jnp.sum(grad_queries.astype(jnp.float32), axis=0)
        value_bias_term = jnp.sum(grad_values.astype(jnp.float32), axis=0)
        query_term = inner_rows(normed, grad_queries)
        key_term = inner_rows(normed, grad_keys)
        value_term = inner_rows(normed, grad_values)
        grad_normed = lax.psum(
            (
                times_transposed(grad_queries, w_query)
                + times_transposed(grad_keys, w_key)
                + times_transposed(grad_values, w_value)
            ).astype(jnp.bfloat16),
            "tp",
        ).astype(jnp.float32)
        _, first_pull = jax.vjp(norm_rows, inputs, norm1_gain, norm1_shift)
        grad_in_norm, first_gain_term, first_shift_term = first_pull(grad_normed)
        input_grads.append((grad_middle + grad_in_norm).astype(jnp.bfloat16))
        head_sums = [
            head_sums[0] + query_bias_term,
            head_sums[1] + value_bias_term,
            head_sums[2] + up_bias_term,
        ]
        fresh = [
            query_term,
            key_term,
            value_term,
            out_term,
            up_term,
            down_term,
            first_gain_term,
            first_shift_term,
            second_gain_term,
            second_shift_term,
            out_bias_term,
            down_bias_term,
        ]
        running = [older + newer for older, newer in zip(running, fresh)]
    final = (
        lax.psum_scatter(
            running[0].astype(jnp.bfloat16), ("fsdp", "ctx"), scatter_dimension=0, tiled=True
        ).astype(jnp.float32),
        lax.psum_scatter(
            running[1].astype(jnp.bfloat16), ("fsdp", "ctx"), scatter_dimension=0, tiled=True
        ).astype(jnp.float32),
        lax.psum_scatter(
            running[2].astype(jnp.bfloat16), ("fsdp", "ctx"), scatter_dimension=0, tiled=True
        ).astype(jnp.float32),
        lax.psum_scatter(
            running[3].astype(jnp.bfloat16), ("fsdp", "ctx"), scatter_dimension=1, tiled=True
        ).astype(jnp.float32),
        lax.psum_scatter(
            running[4].astype(jnp.bfloat16), ("fsdp", "ctx"), scatter_dimension=0, tiled=True
        ).astype(jnp.float32),
        lax.psum_scatter(
            running[5].astype(jnp.bfloat16), ("fsdp", "ctx"), scatter_dimension=1, tiled=True
        ).astype(jnp.float32),
        lax.psum_scatter(
            running[6].astype(jnp.bfloat16), ("fsdp", "ctx"), scatter_dimension=0, tiled=True
        ).astype(jnp.float32),
        lax.psum_scatter(
            running[7].astype(jnp.bfloat16), ("fsdp", "ctx"), scatter_dimension=0, tiled=True
        ).astype(jnp.float32),
        lax.psum_scatter(
            running[8].astype(jnp.bfloat16), ("fsdp", "ctx"), scatter_dimension=0, tiled=True
        ).astype(jnp.float32),
        lax.psum_scatter(
            running[9].astype(jnp.bfloat16), ("fsdp", "ctx"), scatter_dimension=0, tiled=True
        ).astype(jnp.float32),
        lax.psum_scatter(
            running[10].astype(jnp.bfloat16), ("fsdp", "ctx"), scatter_dimension=0, tiled=True
        ).astype(jnp.float32),
        lax.psum_scatter(
            running[11].astype(jnp.bfloat16), ("fsdp", "ctx"), scatter_dimension=0, tiled=True
        ).astype(jnp.float32),
    )
    bias_totals = lax.psum((head_sums[0], head_sums[1], head_sums[2]), ("fsdp", "ctx"))
    return (
        jnp.stack(layer_rows),
        jnp.stack(input_grads),
        final[6],
        final[7],
        final[0],
        bias_totals[0],
        final[1],
        final[2],
        bias_totals[1],
        final[3],
        final[10],
        final[8],
        final[9],
        final[4],
        bias_totals[2],
        final[5],
        final[11],
    )


def solution(mesh):
    in_specs = (
        P("fsdp", "ctx", None),
        P("fsdp", "ctx"),
        P("fsdp", "ctx"),
        P("fsdp", None),
        P(),
        P(),
        P("fsdp", "tp"),
        P("tp"),
        P("fsdp", "tp"),
        P("fsdp", "tp"),
        P("tp"),
        P("tp", "fsdp"),
        P(),
        P(),
        P(),
        P("fsdp", "tp"),
        P("tp"),
        P("tp", "fsdp"),
        P(),
        P("fsdp", "ctx", None),
    )
    out_specs = (
        P("fsdp", "ctx", None),
        P("fsdp", "ctx", None),
        P(("fsdp", "ctx")),
        P(("fsdp", "ctx")),
        P(("fsdp", "ctx"), "tp"),
        P("tp"),
        P(("fsdp", "ctx"), "tp"),
        P(("fsdp", "ctx"), "tp"),
        P("tp"),
        P("tp", ("fsdp", "ctx")),
        P(("fsdp", "ctx")),
        P(("fsdp", "ctx")),
        P(("fsdp", "ctx")),
        P(("fsdp", "ctx"), "tp"),
        P("tp"),
        P("tp", ("fsdp", "ctx")),
        P(("fsdp", "ctx")),
    )
    return jax.shard_map(
        per_device, mesh=mesh, in_specs=in_specs, out_specs=out_specs, check_vma=False
    )
```

profile of v0, /device:TPU:0, one launch (start us, length us, event | category | flops | bytes accessed | tf_op | source)
XLA Modules:
  0.0 1765.6 jit_solution(16813001893812341595)
XLA Ops:
  14.5 30.9 %all-gather.17.cloned.1.call-done = bf16[2048,512]{1,0:T(8,128)(2,1)} async-done(((bf16[1024,512]{1,0:T(8,128)(2,1)}), bf16[2048,512]{1,0:T(8,128)(2,1)}) %all-gather.17.cloned.1.call-update) | async-done | bytes 2097168 | tf_op jit(solution)/shard_map/all_gather | solution.py:67
  49.2 30.9 %all-gather.11.cloned.1.call-done = bf16[2048,512]{1,0:T(8,128)(2,1)} async-done(((bf16[1024,512]{1,0:T(8,128)(2,1)}), bf16[2048,512]{1,0:T(8,128)(2,1)}) %all-gather.11.cloned.1.call-update) | async-done | bytes 2097168 | tf_op jit(solution)/shard_map/all_gather | solution.py:68
  84.4 13.3 all_gather.39
  97.6 13.4 all_gather.38
  118.4 44.0 %all-gather.19.cloned.1.call-done = bf16[2048,512]{1,0:T(8,128)(2,1)} async-done(((bf16[512,512]{1,0:T(8,128)(2,1)}), bf16[2048,512]{1,0:T(8,128)(2,1)}) %all-gather.19.cloned.1.call-update) | async-done | bytes 2097168 | tf_op jit(solution)/shard_map/all_gather | solution.py:114
  182.8 26.1 %all-gather.13.cloned.1.call-done = bf16[2048,512]{1,0:T(8,128)(2,1)} async-done(((bf16[512,512]{1,0:T(8,128)(2,1)}), bf16[2048,512]{1,0:T(8,128)(2,1)}) %all-gather.13.cloned.1.call-update) | async-done | bytes 2097168 | tf_op jit(solution)/shard_map/all_gather | solution.py:115
  217.4 24.8 %all-gather.21.cloned.1.call-done = bf16[512,2048]{1,0:T(8,128)(2,1)} async-done(((bf16[512,1024]{1,0:T(8,128)(2,1)}), bf16[512,2048]{1,0:T(8,128)(2,1)}) %all-gather.21.cloned.1.call-update) | async-done | bytes 2097168 | tf_op jit(solution)/shard_map/all_gather | solution.py:69
  246.9 51.0 %all-reduce.15.cloned.1.call-done = bf16[512,2048]{1,0:T(8,128)(2,1)} async-done(((bf16[512,2048]{1,0:T(8,128)(2,1)}), bf16[512,2048]{1,0:T(8,128)(2,1)}) %all-reduce.15.cloned.1.call-update) | async-done | bytes 2097168 | tf_op jit(solution)/shard_map/psum | solution.py:144
  317.3 35.4 %all-gather.29.cloned.1.call-done = bf16[2048,512]{1,0:T(8,128)(2,1)} async-done(((bf16[512,512]{1,0:T(8,128)(2,1)}), bf16[2048,512]{1,0:T(8,128)(2,1)}) %all-gather.29.cloned.1.call-update) | async-done | bytes 2097168 | tf_op jit(solution)/shard_map/all_gather | solution.py:114
  373.2 26.0 %all-gather.27.cloned.1.call-done = bf16[2048,512]{1,0:T(8,128)(2,1)} async-done(((bf16[512,512]{1,0:T(8,128)(2,1)}), bf16[2048,512]{1,0:T(8,128)(2,1)}) %all-gather.27.cloned.1.call-update) | async-done | bytes 2097168 | tf_op jit(solution)/shard_map/all_gather | solution.py:115
  412.6 48.8 %all-reduce.17.cloned.1.call-done = bf16[512,2048]{1,0:T(8,128)(2,1)} async-done(((bf16[512,2048]{1,0:T(8,128)(2,1)}), bf16[512,2048]{1,0:T(8,128)(2,1)}) %all-reduce.17.cloned.1.call-update) | async-done | bytes 2097168 | tf_op jit(solution)/shard_map/psum | solution.py:144
  467.8 99.3 %all-gather.23.cloned.1.call-done = bf16[2048,2048]{1,0:T(8,128)(2,1)} async-done(((bf16[1024,2048]{1,0:T(8,128)(2,1)}), bf16[2048,2048]{1,0:T(8,128)(2,1)}) %all-gather.23.cloned.1.call-update) | async-done | bytes 8388624 | tf_op jit(solution)/shard_map/all_gather | solution.py:70
  577.3 26.2 %multiply_convert_fusion.5 = (bf16[512,2048]{1,0:T(8,128)(2,1)}, f32[512,2048]{1,0:T(8,128)}, bf16[512,2048]{1,0:T(8,128)(2,1)}, f32[512,2048]{1,0:T(8,128)}, f32[512,2048]{1,0:T(8,128)}) fusion(f32[2048]{0:T(1024)S(1)} %copy-done.101, f32[512,2048]{1,0:T(8,128)S(1)} %fusion.142, bf16[2048,2048]{1,0:T(8,128)(2,1)S(1)} %copy-done.99, ...), kind=kOutput, calls=%fused_computation.131 | convolution fusion | flops 4442816512 | bytes 33591296 | tf_op jit(solution)/shard_map/dot_general | solution.py:151
  603.5 68.9 %all-gather.25.cloned.1.call-done = bf16[2048,2048]{1,0:T(8,128)(2,1)} async-done(((bf16[2048,1024]{1,0:T(8,128)(2,1)}), bf16[2048,2048]{1,0:T(8,128)(2,1)}) %all-gather.25.cloned.1.call-update) | async-done | bytes 8388624 | tf_op jit(solution)/shard_map/all_gather | solution.py:71
  672.5 14.2 convert_reduce_fusion.8
  696.6 12.2 convert_reduce_fusion.9
  719.4 85.0 %all-reduce.21.cloned.1.call-done = (bf16[512,2048]{1,0:T(8,128)(2,1)}, bf16[512,2048]{1,0:T(8,128)(2,1)}) async-done(((bf16[512,2048]{1,0:T(8,128)(2,1)}, bf16[512,2048]{1,0:T(8,128)(2,1)}), (bf16[512,2048]{1,0:T(8,128)(2,1)}, bf16[512,2048]{1,0:T(8,128)(2,1)})) %all-reduce.21.cloned.1.call-update) | async-done | bytes 4194320 | tf_op jit(solution)/shard_map/psum | solution.py:169
  859.2 12.0 multiply_convert_fusion.1
  875.6 11.5 multiply_reduce_fusion
  887.1 11.9 multiply_convert_fusion
  936.5 31.4 %reduce-scatter.11.cloned.1.call-done = bf16[512,512]{0,1:T(8,128)(2,1)} async-done(((bf16[2048,512]{0,1:T(8,128)(2,1)}), bf16[512,512]{0,1:T(8,128)(2,1)}) %reduce-scatter.11.cloned.1.call-update) | async-done | bytes 524304 | tf_op jit(solution)/shard_map/reduce_scatter | solution.py:210
  972.3 40.7 %reduce-scatter.15.cloned.1.call-done = bf16[512,512]{0,1:T(8,128)(2,1)} async-done(((bf16[2048,512]{0,1:T(8,128)(2,1)}), bf16[512,512]{0,1:T(8,128)(2,1)}) %reduce-scatter.15.cloned.1.call-update) | async-done | bytes 524304 | tf_op jit(solution)/shard_map/reduce_scatter | solution.py:210
  1049.6 13.8 fusion.140
  1063.4 15.7 add_convert_fusion.1
  1108.8 46.7 %reduce-scatter.19.cloned.1.call-done = bf16[256,512]{1,0:T(8,128)(2,1)} async-done(((bf16[2048,512]{1,0:T(8,128)(2,1)}), bf16[256,512]{1,0:T(8,128)(2,1)}) %reduce-scatter.19.cloned.1.call-update) | async-done | bytes 262160 | tf_op jit(solution)/shard_map/reduce_scatter | solution.py:256
  1157.3 35.1 %all-reduce.6 = (f32[512]{0:T(512)}, f32[512]{0:T(512)}, f32[2048]{0:T(1024)}) all-reduce(f32[512]{0:T(512)S(1)} %add_bitcast_fusion, f32[512]{0:T(512)S(1)} %add.353, f32[2048]{0:T(1024)S(1)} %add.359), channel_id=1, replica_groups=mesh['fsdp'=2,'ctx'=4,'tp'=4] {'fsdp','ctx'}, use_global_device_ids=true, to_apply=%region_47.48 | all-reduce | flops 3072 | bytes 24576 | tf_op jit(solution)/shard_map/psum | solution.py:293
  1192.4 34.0 %reduce-scatter.23.cloned.1.call-done = bf16[256,512]{1,0:T(8,128)(2,1)} async-done(((bf16[2048,512]{1,0:T(8,128)(2,1)}), bf16[256,512]{1,0:T(8,128)(2,1)}) %reduce-scatter.23.cloned.1.call-update) | async-done | bytes 262160 | tf_op jit(solution)/shard_map/reduce_scatter | solution.py:262
  1228.2 69.2 %reduce-scatter.21.cloned.1.call-done = bf16[256,512]{1,0:T(8,128)(2,1)} async-done(((bf16[2048,512]{1,0:T(8,128)(2,1)}), bf16[256,512]{1,0:T(8,128)(2,1)}) %reduce-scatter.21.cloned.1.call-update) | async-done | bytes 262160 | tf_op jit(solution)/shard_map/reduce_scatter | solution.py:259
  1299.2 153.4 %all-reduce.19.cloned.1.call-done = (bf16[512,2048]{1,0:T(8,128)(2,1)}, bf16[512,2048]{1,0:T(8,128)(2,1)}, bf16[512,2048]{1,0:T(8,128)(2,1)}, bf16[512,2048]{1,0:T(8,128)(2,1)}) async-done(((bf16[512,2048]{1,0:T(8,128)(2,1)}, bf16[512,2048]{1,0:T(8,128)(2,1)}, bf16[512,2048]{1,0:T(8,128)(2,1)}, bf16[512,2048]{1,0:T(8,128)(2,1)}), (bf16[512,2048]{1,0:T(8,128)(2,1)}, bf16[512,2048]{1,0:T(8,128)(2,1)}, ...) | async-done | bytes 8388624 | tf_op jit(solution)/shard_map/psum | solution.py:154
  1462.6 40.6 %all-reduce.7 = (bf16[2048]{0:T(1024)(128)(2,1)S(1)}, bf16[2048]{0:T(1024)(128)(2,1)S(1)}, bf16[2048]{0:T(1024)(128)(2,1)S(1)}, bf16[2048]{0:T(1024)(128)(2,1)S(...) all-reduce(bf16[2048]{0:T(1024)(128)(2,1)S(1)} %add_convert_fusion., ...), channel_id=6, replica_groups=mesh['fsdp'=2,'ctx'=4,'tp'=4] {'fsdp','ctx'}, use_global_device_ids=true, to_apply=%region_40.41.clone | all-reduce | flops 12288 | bytes 49152
  1525.9 79.1 %reduce-scatter.27.cloned.1.call-done = bf16[256,2048]{1,0:T(8,128)(2,1)} async-done(((bf16[2048,2048]{1,0:T(8,128)(2,1)}), bf16[256,2048]{1,0:T(8,128)(2,1)}) %reduce-scatter.27.cloned.1.call-update) | async-done | bytes 1048592 | tf_op jit(solution)/shard_map/reduce_scatter | solution.py:268
  1607.9 147.7 %reduce-scatter.29.cloned.1.call-done = bf16[2048,256]{1,0:T(8,128)(2,1)} async-done(((bf16[2048,2048]{1,0:T(8,128)(2,1)}), bf16[2048,256]{1,0:T(8,128)(2,1)}) %reduce-scatter.29.cloned.1.call-update) | async-done | bytes 1048592 | tf_op jit(solution)/shard_map/reduce_scatter | solution.py:271
  (399 shorter events, 355.5 us)
Async XLA Ops:
  7.2 38.2 %all-gather.17.cloned.1.call-start = ((), (), s32[]{:S(2)}) async-start(), calls=%async_computation.13 | async-start | bytes 3145728 | tf_op jit(solution)/shard_map/all_gather | solution.py:67
  7.9 72.1 %all-gather.11.cloned.1.call-start = ((), (), s32[]{:S(2)}) async-start(), calls=%async_computation.10 | async-start | bytes 3145728 | tf_op jit(solution)/shard_map/all_gather | solution.py:68
  8.7 106.0 %all-gather.15.cloned.1.call-start = ((), (), s32[]{:S(2)}) async-start(), calls=%async_computation.12 | async-start | bytes 3145728 | tf_op jit(solution)/shard_map/all_gather | solution.py:66
  9.4 153.0 %all-gather.19.cloned.1.call-start = ((), (), s32[]{:S(2)}) async-start(), calls=%async_computation.14 | async-start | bytes 2621440 | tf_op jit(solution)/shard_map/all_gather | solution.py:114
  14.5 100.2 %copy-start.27 = (bf16[512,2048]{1,0:T(8,128)(2,1)}, bf16[512,2048]{1,0:T(8,128)(2,1)S(1)}, u32[]{:S(2)}) copy-start(bf16[512,2048]{1,0:T(8,128)(2,1)S(1)} %fusion.33) | copy-start | bytes 6291460
  49.1 159.8 %all-gather.13.cloned.1.call-start = ((), (), s32[]{:S(2)}) async-start(), calls=%async_computation.11 | async-start | bytes 2621440 | tf_op jit(solution)/shard_map/all_gather | solution.py:115
  83.7 158.5 %all-gather.21.cloned.1.call-start = ((), (), s32[]{:S(2)}) async-start(), calls=%async_computation.15 | async-start | bytes 3145728 | tf_op jit(solution)/shard_map/all_gather | solution.py:69
  84.3 213.7 %all-reduce.15.cloned.1.call-start = ((), (), s32[]{:S(2)}) async-start(), calls=%async_computation.16 | async-start | bytes 4194304 | tf_op jit(solution)/shard_map/psum | solution.py:144
  217.4 84.9 %copy-start.52 = (bf16[4,128,512]{2,1,0:T(8,128)(2,1)}, bf16[4,128,512]{2,1,0:T(8,128)(2,1)S(1)}, u32[]{:S(2)}) copy-start(bf16[4,128,512]{2,1,0:T(8,128)(2,1)S(1)} %fusion.127) | copy-start | bytes 1572868
  217.4 80.6 %copy-start.51 = (f32[2048]{0:T(1024)S(1)}, f32[2048]{0:T(1024)}, u32[]{:S(2)}) copy-start(f32[2048]{0:T(1024)} %param.32) | copy-start | bytes 24580
  246.5 106.1 %all-gather.29.cloned.1.call-start = ((), (), s32[]{:S(2)}) async-start(), calls=%async_computation.20 | async-start | bytes 2621440 | tf_op jit(solution)/shard_map/all_gather | solution.py:114
  306.7 92.5 %all-gather.27.cloned.1.call-start = ((), (), s32[]{:S(2)}) async-start(), calls=%async_computation.19 | async-start | bytes 2621440 | tf_op jit(solution)/shard_map/all_gather | solution.py:115
  310.5 150.9 %all-reduce.17.cloned.1.call-start = ((), (), s32[]{:S(2)}) async-start(), calls=%async_computation.21 | async-start | bytes 4194304 | tf_op jit(solution)/shard_map/psum | solution.py:144
  411.0 156.0 %all-gather.23.cloned.1.call-start = ((), (), s32[]{:S(2)}) async-start(), calls=%async_computation.17 | async-start | bytes 12582912 | tf_op jit(solution)/shard_map/all_gather | solution.py:70
  411.8 260.7 %all-gather.25.cloned.1.call-start = ((), (), s32[]{:S(2)}) async-start(), calls=%async_computation.18 | async-start | bytes 12582912 | tf_op jit(solution)/shard_map/all_gather | solution.py:71
  412.3 392.0 %all-reduce.21.cloned.1.call-start = ((), (), s32[]{:S(2)}) async-start(), calls=%async_computation.33 | async-start | bytes 8388608 | tf_op jit(solution)/shard_map/psum | solution.py:169
  465.9 101.2 %copy-start.56 = (f32[2048]{0:T(1024)S(1)}, f32[2048]{0:T(1024)}, u32[]{:S(2)}) copy-start(f32[2048]{0:T(1024)} %param.33) | copy-start | bytes 24580
  465.9 101.2 %copy-start.102 = (f32[2048]{0:T(1024)S(1)}, f32[2048]{0:T(1024)}, u32[]{:S(2)}) copy-start(f32[2048]{0:T(1024)} %param.34) | copy-start | bytes 24580
  465.9 351.3 %copy-start.59 = (f32[512]{0:T(512)}, f32[512]{0:T(512)S(1)}, u32[]{:S(2)}) copy-start(f32[512]{0:T(512)S(1)} %get-tuple-element.104) | copy-start | bytes 6148
  467.8 349.4 %copy-start.74 = (f32[512]{0:T(512)}, f32[512]{0:T(512)S(1)}, u32[]{:S(2)}) copy-start(f32[512]{0:T(512)S(1)} %fusion.137) | copy-start | bytes 6148
  467.8 109.5 %copy-start.101 = (f32[2048]{0:T(1024)S(1)}, f32[2048]{0:T(1024)}, u32[]{:S(2)}) copy-start(f32[2048]{0:T(1024)} %param.36) | copy-start | bytes 24580
  718.7 207.5 %reduce-scatter.13.cloned.1.call-start = ((), (), s32[]{:S(2)}) async-start(), calls=%async_computation.23 | async-start | bytes 2621440 | tf_op jit(solution)/shard_map/reduce_scatter | solution.py:213
  834.0 96.5 %reduce-scatter.17.cloned.1.call-start = ((), (), s32[]{:S(2)}) async-start(), calls=%async_computation.25 | async-start | bytes 2621440 | tf_op jit(solution)/shard_map/reduce_scatter | solution.py:213
  847.8 120.1 %reduce-scatter.11.cloned.1.call-start = ((), (), s32[]{:S(2)}) async-start(), calls=%async_computation.22 | async-start | bytes 2621440 | tf_op jit(solution)/shard_map/reduce_scatter | solution.py:210
  875.5 137.4 %reduce-scatter.15.cloned.1.call-start = ((), (), s32[]{:S(2)}) async-start(), calls=%async_computation.24 | async-start | bytes 2621440 | tf_op jit(solution)/shard_map/reduce_scatter | solution.py:210
  903.5 203.5 %reduce-scatter.25.cloned.1.call-start = ((), (), s32[]{:S(2)}) async-start(), calls=%async_computation.29 | async-start | bytes 2359296 | tf_op jit(solution)/shard_map/reduce_scatter | solution.py:265
  908.0 247.5 %reduce-scatter.19.cloned.1.call-start = ((), (), s32[]{:S(2)}) async-start(), calls=%async_computation.26 | async-start | bytes 2359296 | tf_op jit(solution)/shard_map/reduce_scatter | solution.py:256
  926.1 300.4 %reduce-scatter.23.cloned.1.call-start = ((), (), s32[]{:S(2)}) async-start(), calls=%async_computation.28 | async-start | bytes 2359296 | tf_op jit(solution)/shard_map/reduce_scatter | solution.py:262
  936.5 361.0 %reduce-scatter.21.cloned.1.call-start = ((), (), s32[]{:S(2)}) async-start(), calls=%async_computation.27 | async-start | bytes 2359296 | tf_op jit(solution)/shard_map/reduce_scatter | solution.py:259
  1018.8 433.8 %all-reduce.19.cloned.1.call-start = ((), (), s32[]{:S(2)}) async-start(), calls=%async_computation.32 | async-start | bytes 16777216 | tf_op jit(solution)/shard_map/psum | solution.py:154
  1048.9 556.1 %reduce-scatter.27.cloned.1.call-start = ((), (), s32[]{:S(2)}) async-start(), calls=%async_computation.30 | async-start | bytes 9437184 | tf_op jit(solution)/shard_map/reduce_scatter | solution.py:268
  1079.1 676.5 %reduce-scatter.29.cloned.1.call-start = ((), (), s32[]{:S(2)}) async-start(), calls=%async_computation.31 | async-start | bytes 9437184 | tf_op jit(solution)/shard_map/reduce_scatter | solution.py:271
  (108 other events, 1377.4 us)
Sparse Core Ops, SparseCore 0:
  9.5 35.8 all-gather.16
  46.9 33.0 all-gather.10
  81.6 33.0 all-gather.14
  116.7 45.6 all-gather.18
  164.4 44.4 all-gather.12
  210.3 31.8 all-gather.20
  246.6 51.3 all-reduce.14
  306.8 45.7 all-gather.28
  354.8 44.4 all-gather.26
  411.1 50.1 all-reduce.16
  462.9 104.0 all-gather.22
  568.4 103.9 all-gather.24
  718.8 85.5 all-reduce.20
  834.1 43.7 reduce-scatter.12
  880.1 42.8 reduce-scatter.16
  925.1 42.8 reduce-scatter.10
  970.1 42.8 reduce-scatter.14
  1016.3 68.1 reduce-scatter.24
  1088.0 67.4 reduce-scatter.18
  1158.9 67.5 reduce-scatter.22
  1230.0 67.3 reduce-scatter.20
  1300.7 151.8 all-reduce.18
  1456.2 148.7 reduce-scatter.26
  1608.6 146.9 reduce-scatter.28
where the time goes:
time: 1770 us
  waiting for transfers between devices  1180 us (67%)
  matrix products  317 us (18%)
  other arithmetic  126 us (7%)
  blocking collectives  102 us (6%)
  local copies, waits for them, and re-layouts  21.5 us (1%)
    psum x1, waiting for transfers between devices, per_device(): lax.psum(jnp.dot(active, w_down, preferred_element_type=jnp.float32).asty...  153 us
    reduce_scatter x1, waiting for transfers between devices, per_device(): lax.psum_scatter(running[5].astype(jnp.bfloat16), ('fsdp', 'ctx'), scatte...  148 us
    psum x2, waiting for transfers between devices, per_device(): lax.psum(jnp.dot(attended, w_out, preferred_element_type=jnp.float32).ast...  99.8 us
    all_gather x1, waiting for transfers between devices, per_device(): lax.all_gather(up_weight, 'fsdp', axis=0, tiled=True)  99.3 us
    psum x1, waiting for transfers between devices, per_device(): lax.psum(times_transposed(grad_hidden, w_up).astype(jnp.bfloat16), 'tp')  85 us
    all_gather x2, waiting for transfers between devices, per_device(): lax.all_gather(keys_local, 'ctx', axis=0, tiled=True)  79.4 us
    dot_general x12, matrix products, inner_rows(): lax.dot_general(left, right, (((0,), (0,)), ((), ())), preferred_element_...  79.2 us
    reduce_scatter x1, waiting for transfers between devices, per_device(): lax.psum_scatter(running[4].astype(jnp.bfloat16), ('fsdp', 'ctx'), scatte...  79.1 us
  transfers between devices with their start and end apart: 24, of which 21 were waited for; matrix products, arithmetic and copies ran while one was open for 20% of the time, Pallas kernels for 0%

commit v1 on v0

--- a/solution.py
+++ b/solution.py
@@ -7,6 +7,28 @@
 
 HD = 128
 NEGATIVE = -1000000000.0
+
+
+def in_order(parts, dim):
+    parts = jnp.moveaxis(parts, 0, dim)
+    shape = parts.shape
+    return parts.reshape(*shape[:dim], shape[dim] * shape[dim + 1], *shape[dim + 2 :])
+
+
+def collected_by_bits(array, axis):
+    size = lax.axis_size(axis)
+    parts = array[None]
+    for level in range(size.bit_length() - 1):
+        bit = 1 << level
+        other = lax.ppermute(parts, axis, [(i, i ^ bit) for i in range(size)])
+        both = jnp.stack([parts, other])
+        upper = lax.axis_index(axis) >> level & 1
+        parts = jnp.where(upper == 0, both, both[::-1]).reshape(-1, *array.shape)
+    return parts
+
+
+def gather_by_bits(x, axis, dim):
+    return in_order(collected_by_bits(x, axis), dim)
 
 
 def norm_rows(values, gain, shift):
@@ -67,7 +89,7 @@
         lax.all_gather(key_weight, "fsdp", axis=0, tiled=True),
         lax.all_gather(value_weight, "fsdp", axis=0, tiled=True),
         lax.all_gather(out_weight, "fsdp", axis=1, tiled=True),
-        lax.all_gather(up_weight, "fsdp", axis=0, tiled=True),
+        gather_by_bits(up_weight, "fsdp", 0),
         lax.all_gather(down_weight, "fsdp", axis=1, tiled=True),
     )
     key_position, key_segment = (

time: 1770 us -> 1660 us (0.938)
  waiting for transfers between devices: 1180 us -> 1050 us
  other arithmetic: 126 us -> 148 us
    all_gather x1 -> x0, waiting for transfers between devices: 99.3 us -> none  [per_device(): lax.all_gather(up_weight, 'fsdp', axis=0, tiled=True)]
    psum x2, waiting for transfers between devices: 99.8 us -> 78.3 us  [per_device(): lax.psum(jnp.dot(attended, w_out, preferred_element_type=jnp.float32).ast...]
  transfers between devices with their start and end apart: 24 -> 24, of which waited for: 21 -> 20; matrix products, arithmetic and copies ran while one was open for 20% -> 23% of each run, Pallas kernels for 0% -> 0%
where the time goes in v1:
time: 1660 us
  waiting for transfers between devices  1050 us (63%)
  matrix products  317 us (19%)
  other arithmetic  148 us (9%)
  blocking collectives  103 us (6%)
  local copies, waits for them, and re-layouts  21.3 us (1%)
  between operations  16.7 us (1%)
    psum x1, waiting for transfers between devices, per_device(): lax.psum(jnp.dot(active, w_down, preferred_element_type=jnp.float32).asty...  153 us
    reduce_scatter x1, waiting for transfers between devices, per_device(): lax.psum_scatter(running[5].astype(jnp.bfloat16), ('fsdp', 'ctx'), scatte...  148 us
    psum x1, waiting for transfers between devices, per_device(): lax.psum(times_transposed(grad_hidden, w_up).astype(jnp.bfloat16), 'tp')  85 us
    dot_general x12, matrix products, inner_rows(): lax.dot_general(left, right, (((0,), (0,)), ((), ())), preferred_element_...  79.2 us
    reduce_scatter x1, waiting for transfers between devices, per_device(): lax.psum_scatter(running[4].astype(jnp.bfloat16), ('fsdp', 'ctx'), scatte...  79.2 us
    psum x2, waiting for transfers between devices, per_device(): lax.psum(jnp.dot(attended, w_out, preferred_element_type=jnp.float32).ast...  78.3 us
    all_gather x2, waiting for transfers between devices, per_device(): lax.all_gather(keys_local, 'ctx', axis=0, tiled=True)  77.9 us
    reduce_scatter x2, waiting for transfers between devices, per_device(): lax.psum_scatter(key_part.astype(jnp.bfloat16), 'ctx', scatter_dimension=...  72 us
  transfers between devices with their start and end apart: 24, of which 20 were waited for; matrix products, arithmetic and copies ran while one was open for 23% of the time, Pallas kernels for 0%

profile of v1, /device:TPU:0, one launch (start us, length us, event | category | flops | bytes accessed | tf_op | source)
XLA Modules:
  0.0 1660.0 jit_solution(9006748655891074867)
XLA Ops:
  14.5 30.9 %all-gather.16.cloned.1.call-done = bf16[2048,512]{1,0:T(8,128)(2,1)} async-done(((bf16[1024,512]{1,0:T(8,128)(2,1)}), bf16[2048,512]{1,0:T(8,128)(2,1)}) %all-gather.16.cloned.1.call-update) | async-done | bytes 2097168 | tf_op jit(solution)/shard_map/all_gather | solution.py:89
  49.2 30.9 %all-gather.10.cloned.1.call-done = bf16[2048,512]{1,0:T(8,128)(2,1)} async-done(((bf16[1024,512]{1,0:T(8,128)(2,1)}), bf16[2048,512]{1,0:T(8,128)(2,1)}) %all-gather.10.cloned.1.call-update) | async-done | bytes 2097168 | tf_op jit(solution)/shard_map/all_gather | solution.py:90
  84.4 13.3 all_gather.36
  97.6 13.7 all_gather.35
  118.4 44.0 %all-gather.18.cloned.1.call-done = bf16[2048,512]{1,0:T(8,128)(2,1)} async-done(((bf16[512,512]{1,0:T(8,128)(2,1)}), bf16[2048,512]{1,0:T(8,128)(2,1)}) %all-gather.18.cloned.1.call-update) | async-done | bytes 2097168 | tf_op jit(solution)/shard_map/all_gather | solution.py:136
  182.8 26.1 %all-gather.12.cloned.1.call-done = bf16[2048,512]{1,0:T(8,128)(2,1)} async-done(((bf16[512,512]{1,0:T(8,128)(2,1)}), bf16[2048,512]{1,0:T(8,128)(2,1)}) %all-gather.12.cloned.1.call-update) | async-done | bytes 2097168 | tf_op jit(solution)/shard_map/all_gather | solution.py:137
  217.4 24.8 %all-gather.20.cloned.1.call-done = bf16[512,2048]{1,0:T(8,128)(2,1)} async-done(((bf16[512,1024]{1,0:T(8,128)(2,1)}), bf16[512,2048]{1,0:T(8,128)(2,1)}) %all-gather.20.cloned.1.call-update) | async-done | bytes 2097168 | tf_op jit(solution)/shard_map/all_gather | solution.py:91
  246.7 51.3 %all-reduce.15.cloned.1.call-done = bf16[512,2048]{1,0:T(8,128)(2,1)} async-done(((bf16[512,2048]{1,0:T(8,128)(2,1)}), bf16[512,2048]{1,0:T(8,128)(2,1)}) %all-reduce.15.cloned.1.call-update) | async-done | bytes 2097168 | tf_op jit(solution)/shard_map/psum | solution.py:166
  318.8 33.9 %all-gather.26.cloned.1.call-done = bf16[2048,512]{1,0:T(8,128)(2,1)} async-done(((bf16[512,512]{1,0:T(8,128)(2,1)}), bf16[2048,512]{1,0:T(8,128)(2,1)}) %all-gather.26.cloned.1.call-update) | async-done | bytes 2097168 | tf_op jit(solution)/shard_map/all_gather | solution.py:136
  373.3 26.0 %all-gather.24.cloned.1.call-done = bf16[2048,512]{1,0:T(8,128)(2,1)} async-done(((bf16[512,512]{1,0:T(8,128)(2,1)}), bf16[2048,512]{1,0:T(8,128)(2,1)}) %all-gather.24.cloned.1.call-update) | async-done | bytes 2097168 | tf_op jit(solution)/shard_map/all_gather | solution.py:137
  420.0 14.4 reverse_select_fusion
  434.4 27.1 %all-reduce.17.cloned.1.call-done = bf16[512,2048]{1,0:T(8,128)(2,1)} async-done(((bf16[512,2048]{1,0:T(8,128)(2,1)}), bf16[512,2048]{1,0:T(8,128)(2,1)}) %all-reduce.17.cloned.1.call-update) | async-done | bytes 2097168 | tf_op jit(solution)/shard_map/psum | solution.py:166
  478.1 26.2 %multiply_convert_fusion.5 = (bf16[512,2048]{1,0:T(8,128)(2,1)}, f32[512,2048]{1,0:T(8,128)}, bf16[512,2048]{1,0:T(8,128)(2,1)}, f32[512,2048]{1,0:T(8,128)}, f32[512,2048]{1,0:T(8,128)}) fusion(f32[2048]{0:T(1024)S(1)} %copy-done.103, f32[512,2048]{1,0:T(8,128)S(1)} %fusion.142, bf16[2048,2048]{1,0:T(8,128)(2,1)S(1)} %bitcast.344, ...), kind=kOutput, calls=%fused_computation.133 | convolution fusion | flops 4442816512 | bytes 33591296 | tf_op jit(solution)/shard_map/dot_general | solution.py:173
  504.3 62.8 %all-gather.22.cloned.1.call-done = bf16[2048,2048]{1,0:T(8,128)(2,1)} async-done(((bf16[2048,1024]{1,0:T(8,128)(2,1)}), bf16[2048,2048]{1,0:T(8,128)(2,1)}) %all-gather.22.cloned.1.call-update) | async-done | bytes 8388624 | tf_op jit(solution)/shard_map/all_gather | solution.py:93
  567.1 14.1 convert_reduce_fusion.8
  591.3 12.1 convert_reduce_fusion.9
  614.0 85.0 %all-reduce.21.cloned.1.call-done = (bf16[512,2048]{1,0:T(8,128)(2,1)}, bf16[512,2048]{1,0:T(8,128)(2,1)}) async-done(((bf16[512,2048]{1,0:T(8,128)(2,1)}, bf16[512,2048]{1,0:T(8,128)(2,1)}), (bf16[512,2048]{1,0:T(8,128)(2,1)}, bf16[512,2048]{1,0:T(8,128)(2,1)})) %all-reduce.21.cloned.1.call-update) | async-done | bytes 4194320 | tf_op jit(solution)/shard_map/psum | solution.py:191
  753.9 12.0 multiply_convert_fusion.1
  770.2 11.6 multiply_reduce_fusion
  781.8 11.9 multiply_convert_fusion
  831.2 31.4 %reduce-scatter.11.cloned.1.call-done = bf16[512,512]{0,1:T(8,128)(2,1)} async-done(((bf16[2048,512]{0,1:T(8,128)(2,1)}), bf16[512,512]{0,1:T(8,128)(2,1)}) %reduce-scatter.11.cloned.1.call-update) | async-done | bytes 524304 | tf_op jit(solution)/shard_map/reduce_scatter | solution.py:232
  866.9 40.6 %reduce-scatter.15.cloned.1.call-done = bf16[512,512]{0,1:T(8,128)(2,1)} async-done(((bf16[2048,512]{0,1:T(8,128)(2,1)}), bf16[512,512]{0,1:T(8,128)(2,1)}) %reduce-scatter.15.cloned.1.call-update) | async-done | bytes 524304 | tf_op jit(solution)/shard_map/reduce_scatter | solution.py:232
  944.2 13.8 fusion.140
  957.9 15.7 add_convert_fusion.1
  1003.4 46.5 %reduce-scatter.19.cloned.1.call-done = bf16[256,512]{1,0:T(8,128)(2,1)} async-done(((bf16[2048,512]{1,0:T(8,128)(2,1)}), bf16[256,512]{1,0:T(8,128)(2,1)}) %reduce-scatter.19.cloned.1.call-update) | async-done | bytes 262160 | tf_op jit(solution)/shard_map/reduce_scatter | solution.py:278
  1051.7 35.2 %all-reduce.6 = (f32[512]{0:T(512)}, f32[512]{0:T(512)}, f32[2048]{0:T(1024)}) all-reduce(f32[512]{0:T(512)S(1)} %add_bitcast_fusion, f32[512]{0:T(512)S(1)} %add.353, f32[2048]{0:T(1024)S(1)} %add.359), channel_id=1, replica_groups=mesh['fsdp'=2,'ctx'=4,'tp'=4] {'fsdp','ctx'}, use_global_device_ids=true, to_apply=%region_47.48 | all-reduce | flops 3072 | bytes 24576 | tf_op jit(solution)/shard_map/psum | solution.py:315
  1087.0 34.2 %reduce-scatter.23.cloned.1.call-done = bf16[256,512]{1,0:T(8,128)(2,1)} async-done(((bf16[2048,512]{1,0:T(8,128)(2,1)}), bf16[256,512]{1,0:T(8,128)(2,1)}) %reduce-scatter.23.cloned.1.call-update) | async-done | bytes 262160 | tf_op jit(solution)/shard_map/reduce_scatter | solution.py:284
  1123.0 69.0 %reduce-scatter.21.cloned.1.call-done = bf16[256,512]{1,0:T(8,128)(2,1)} async-done(((bf16[2048,512]{1,0:T(8,128)(2,1)}), bf16[256,512]{1,0:T(8,128)(2,1)}) %reduce-scatter.21.cloned.1.call-update) | async-done | bytes 262160 | tf_op jit(solution)/shard_map/reduce_scatter | solution.py:281
  1193.8 153.4 %all-reduce.19.cloned.1.call-done = (bf16[512,2048]{1,0:T(8,128)(2,1)}, bf16[512,2048]{1,0:T(8,128)(2,1)}, bf16[512,2048]{1,0:T(8,128)(2,1)}, bf16[512,2048]{1,0:T(8,128)(2,1)}) async-done(((bf16[512,2048]{1,0:T(8,128)(2,1)}, bf16[512,2048]{1,0:T(8,128)(2,1)}, bf16[512,2048]{1,0:T(8,128)(2,1)}, bf16[512,2048]{1,0:T(8,128)(2,1)}), (bf16[512,2048]{1,0:T(8,128)(2,1)}, bf16[512,2048]{1,0:T(8,128)(2,1)}, ...) | async-done | bytes 8388624 | tf_op jit(solution)/shard_map/psum | solution.py:176
  1357.2 40.6 %all-reduce.7 = (bf16[2048]{0:T(1024)(128)(2,1)S(1)}, bf16[2048]{0:T(1024)(128)(2,1)S(1)}, bf16[2048]{0:T(1024)(128)(2,1)S(1)}, bf16[2048]{0:T(1024)(128)(2,1)S(...) all-reduce(bf16[2048]{0:T(1024)(128)(2,1)S(1)} %add_convert_fusion., ...), channel_id=6, replica_groups=mesh['fsdp'=2,'ctx'=4,'tp'=4] {'fsdp','ctx'}, use_global_device_ids=true, to_apply=%region_40.41.clone | all-reduce | flops 12288 | bytes 49152
  1420.5 79.2 %reduce-scatter.27.cloned.1.call-done = bf16[256,2048]{1,0:T(8,128)(2,1)} async-done(((bf16[2048,2048]{1,0:T(8,128)(2,1)}), bf16[256,2048]{1,0:T(8,128)(2,1)}) %reduce-scatter.27.cloned.1.call-update) | async-done | bytes 1048592 | tf_op jit(solution)/shard_map/reduce_scatter | solution.py:290
  1502.5 147.9 %reduce-scatter.29.cloned.1.call-done = bf16[2048,256]{1,0:T(8,128)(2,1)} async-done(((bf16[2048,2048]{1,0:T(8,128)(2,1)}), bf16[2048,256]{1,0:T(8,128)(2,1)}) %reduce-scatter.29.cloned.1.call-update) | async-done | bytes 1048592 | tf_op jit(solution)/shard_map/reduce_scatter | solution.py:293
  (409 shorter events, 363.8 us)
Async XLA Ops:
  7.2 38.2 %all-gather.16.cloned.1.call-start = ((), (), s32[]{:S(2)}) async-start(), calls=%async_computation.13 | async-start | bytes 3145728 | tf_op jit(solution)/shard_map/all_gather | solution.py:89
  7.9 72.1 %all-gather.10.cloned.1.call-start = ((), (), s32[]{:S(2)}) async-start(), calls=%async_computation.10 | async-start | bytes 3145728 | tf_op jit(solution)/shard_map/all_gather | solution.py:90
  8.7 106.0 %all-gather.14.cloned.1.call-start = ((), (), s32[]{:S(2)}) async-start(), calls=%async_computation.12 | async-start | bytes 3145728 | tf_op jit(solution)/shard_map/all_gather | solution.py:88
  9.4 153.0 %all-gather.18.cloned.1.call-start = ((), (), s32[]{:S(2)}) async-start(), calls=%async_computation.14 | async-start | bytes 2621440 | tf_op jit(solution)/shard_map/all_gather | solution.py:136
  14.5 100.2 %copy-start.26 = (bf16[512,2048]{1,0:T(8,128)(2,1)}, bf16[512,2048]{1,0:T(8,128)(2,1)S(1)}, u32[]{:S(2)}) copy-start(bf16[512,2048]{1,0:T(8,128)(2,1)S(1)} %fusion.33) | copy-start | bytes 6291460
  14.5 65.5 %copy-start.106 = (f32[512]{0:T(512)S(1)}, f32[512]{0:T(512)}, u32[]{:S(2)}) copy-start(f32[512]{0:T(512)} %param.30) | copy-start | bytes 6148
  49.1 65.6 %copy-start.107 = (f32[512]{0:T(512)S(1)}, f32[512]{0:T(512)}, u32[]{:S(2)}) copy-start(f32[512]{0:T(512)} %param.27) | copy-start | bytes 6148
  49.1 159.8 %all-gather.12.cloned.1.call-start = ((), (), s32[]{:S(2)}) async-start(), calls=%async_computation.11 | async-start | bytes 2621440 | tf_op jit(solution)/shard_map/all_gather | solution.py:137
  83.7 158.5 %all-gather.20.cloned.1.call-start = ((), (), s32[]{:S(2)}) async-start(), calls=%async_computation.15 | async-start | bytes 3145728 | tf_op jit(solution)/shard_map/all_gather | solution.py:91
  84.3 213.7 %all-reduce.15.cloned.1.call-start = ((), (), s32[]{:S(2)}) async-start(), calls=%async_computation.16 | async-start | bytes 4194304 | tf_op jit(solution)/shard_map/psum | solution.py:166
  217.4 84.9 %copy-start.51 = (bf16[4,128,512]{2,1,0:T(8,128)(2,1)}, bf16[4,128,512]{2,1,0:T(8,128)(2,1)S(1)}, u32[]{:S(2)}) copy-start(bf16[4,128,512]{2,1,0:T(8,128)(2,1)S(1)} %fusion.127) | copy-start | bytes 1572868
  217.4 80.6 %copy-start.50 = (f32[2048]{0:T(1024)S(1)}, f32[2048]{0:T(1024)}, u32[]{:S(2)}) copy-start(f32[2048]{0:T(1024)} %param.32) | copy-start | bytes 24580
  246.5 106.2 %all-gather.26.cloned.1.call-start = ((), (), s32[]{:S(2)}) async-start(), calls=%async_computation.19 | async-start | bytes 2621440 | tf_op jit(solution)/shard_map/all_gather | solution.py:136
  246.7 67.3 %copy-start.64 = (f32[512]{0:T(512)}, f32[512]{0:T(512)S(1)}, u32[]{:S(2)}) copy-start(f32[512]{0:T(512)S(1)} %broadcast_multiply_fusion.1) | copy-start | bytes 6148
  306.8 92.6 %all-gather.24.cloned.1.call-start = ((), (), s32[]{:S(2)}) async-start(), calls=%async_computation.18 | async-start | bytes 2621440 | tf_op jit(solution)/shard_map/all_gather | solution.py:137
  310.5 150.9 %all-reduce.17.cloned.1.call-start = ((), (), s32[]{:S(2)}) async-start(), calls=%async_computation.20 | async-start | bytes 4194304 | tf_op jit(solution)/shard_map/psum | solution.py:166
  310.6 101.7 %collective-permute-start = (bf16[1,1024,2048]{2,1,0:T(8,128)(2,1)}, bf16[1,1024,2048]{2,1,0:T(8,128)(2,1)}, u32[]{:S(2)}, u32[]{:S(2)}) collective-permute-start(bf16[1,1024,2048]{2,1,0:T(8,128)(2,1)} %bitcast.353), channel_id=1, source_target_pairs={{0,16},{16,0},{1,17},{17,1},{2,18},{18,2},{3,19},{19,3},{4,20},{20... | collective-permute-start | bytes 12582920 | tf_op jit(solution)/shard_map/ppermute | solution.py:23
  411.1 156.0 %all-gather.22.cloned.1.call-start = ((), (), s32[]{:S(2)}) async-start(), calls=%async_computation.17 | async-start | bytes 12582912 | tf_op jit(solution)/shard_map/all_gather | solution.py:93
  411.9 287.1 %all-reduce.21.cloned.1.call-start = ((), (), s32[]{:S(2)}) async-start(), calls=%async_computation.32 | async-start | bytes 8388608 | tf_op jit(solution)/shard_map/psum | solution.py:191
  466.0 245.8 %copy-start.60 = (f32[512]{0:T(512)}, f32[512]{0:T(512)S(1)}, u32[]{:S(2)}) copy-start(f32[512]{0:T(512)S(1)} %get-tuple-element.104) | copy-start | bytes 6148
  467.9 243.9 %copy-start.77 = (f32[512]{0:T(512)}, f32[512]{0:T(512)S(1)}, u32[]{:S(2)}) copy-start(f32[512]{0:T(512)S(1)} %fusion.137) | copy-start | bytes 6148
  613.3 207.6 %reduce-scatter.13.cloned.1.call-start = ((), (), s32[]{:S(2)}) async-start(), calls=%async_computation.22 | async-start | bytes 2621440 | tf_op jit(solution)/shard_map/reduce_scatter | solution.py:235
  728.6 96.6 %reduce-scatter.17.cloned.1.call-start = ((), (), s32[]{:S(2)}) async-start(), calls=%async_computation.24 | async-start | bytes 2621440 | tf_op jit(solution)/shard_map/reduce_scatter | solution.py:235
  742.4 120.1 %reduce-scatter.11.cloned.1.call-start = ((), (), s32[]{:S(2)}) async-start(), calls=%async_computation.21 | async-start | bytes 2621440 | tf_op jit(solution)/shard_map/reduce_scatter | solution.py:232
  770.2 137.4 %reduce-scatter.15.cloned.1.call-start = ((), (), s32[]{:S(2)}) async-start(), calls=%async_computation.23 | async-start | bytes 2621440 | tf_op jit(solution)/shard_map/reduce_scatter | solution.py:232
  798.2 203.4 %reduce-scatter.25.cloned.1.call-start = ((), (), s32[]{:S(2)}) async-start(), calls=%async_computation.28 | async-start | bytes 2359296 | tf_op jit(solution)/shard_map/reduce_scatter | solution.py:287
  802.8 247.2 %reduce-scatter.19.cloned.1.call-start = ((), (), s32[]{:S(2)}) async-start(), calls=%async_computation.25 | async-start | bytes 2359296 | tf_op jit(solution)/shard_map/reduce_scatter | solution.py:278
  820.8 300.4 %reduce-scatter.23.cloned.1.call-start = ((), (), s32[]{:S(2)}) async-start(), calls=%async_computation.27 | async-start | bytes 2359296 | tf_op jit(solution)/shard_map/reduce_scatter | solution.py:284
  831.1 360.9 %reduce-scatter.21.cloned.1.call-start = ((), (), s32[]{:S(2)}) async-start(), calls=%async_computation.26 | async-start | bytes 2359296 | tf_op jit(solution)/shard_map/reduce_scatter | solution.py:281
  913.4 433.7 %all-reduce.19.cloned.1.call-start = ((), (), s32[]{:S(2)}) async-start(), calls=%async_computation.31 | async-start | bytes 16777216 | tf_op jit(solution)/shard_map/psum | solution.py:176
  943.5 556.2 %reduce-scatter.27.cloned.1.call-start = ((), (), s32[]{:S(2)}) async-start(), calls=%async_computation.29 | async-start | bytes 9437184 | tf_op jit(solution)/shard_map/reduce_scatter | solution.py:290
  973.7 676.6 %reduce-scatter.29.cloned.1.call-start = ((), (), s32[]{:S(2)}) async-start(), calls=%async_computation.30 | async-start | bytes 9437184 | tf_op jit(solution)/shard_map/reduce_scatter | solution.py:293
  (112 other events, 1275.2 us)
Sparse Core Ops, SparseCore 0:
  9.5 35.8 all-gather.15
  46.9 33.0 all-gather.9
  81.6 33.0 all-gather.13
  116.7 45.6 all-gather.17
  164.4 44.4 all-gather.11
  210.3 31.8 all-gather.19
  246.6 51.3 all-reduce.14
  306.9 45.7 all-gather.25
  354.8 44.4 all-gather.23
  411.2 50.1 all-reduce.16
  463.0 104.0 all-gather.21
  613.4 85.5 all-reduce.20
  728.7 43.7 reduce-scatter.12
  774.7 42.8 reduce-scatter.16
  819.7 42.8 reduce-scatter.10
  864.7 42.8 reduce-scatter.14
  911.0 68.1 reduce-scatter.24
  982.5 67.3 reduce-scatter.18
  1053.4 67.6 reduce-scatter.22
  1124.5 67.3 reduce-scatter.20
  1195.3 151.8 all-reduce.18
  1350.8 148.8 reduce-scatter.26
  1503.3 146.9 reduce-scatter.28
